TPU v7x, 32 devices: a whole 2x2x4 slice. The times are simulated.
32 devices in a mesh: row: 2 (over x), col: 16 (over z, y, core).
Axes of the slice: x: 2, y: 2, z: 4, core: 2. Of those that a mesh axis runs over, the one named last changes fastest.
Arguments:
- activations: bfloat16 [128, 8192], P('col', 'row'), may hold values from -6 to 6
- up_weight: bfloat16 [8192, 53248], P('row', 'col'), may hold values from -0.0625 to 0.0625
- out_grad: bfloat16 [128, 53248], P('row', 'col'), may hold values from -6 to 6
- round_seed: int32 [1], replicated, may hold values from 0 to 1073741823
- counter_base: int32 [128], P('row'), may hold values from 0 to 1073741823
Outputs:
- weight_grad: float32 [8192, 53248], P('row', 'col')
- input_grad: bfloat16 [128, 8192], P('col', 'row')
All inputs are finite; a program needn't handle non-finite values.
Results may differ from a plain program's by a relative error of at most 0.015.
Values may be sent and summed in bfloat16 or wider, within the bound.
No kernel may reach another device: no remote copies, remote signals or barrier semaphores. Data moves between devices by JAX's collectives and lax.ppermute only.
A program may use at most 192 MiB of HBM per device.

v0:
```python
import functools

import jax
import jax.numpy as jnp
from jax import lax
from jax.experimental import pallas as pl
from jax.experimental.pallas import tpu as pltpu
from jax.sharding import PartitionSpec as P


CORES = 2
LANES = 256
MIB = 2**20


def round_kernel(per_col, cuts, seed_ref, base_hbm, grad_hbm, x_hbm, w_hbm, *refs):
    n_cut = len(cuts) - 1
    out_refs, refs = refs[:n_cut], refs[n_cut:]
    copies_hbm, head_ref, base_ref, grad_ref, x_ref, sems, copy_sems = refs
    loads = [
        pltpu.make_async_copy(x_hbm, x_ref, sems.at[0]),
        pltpu.make_async_copy(base_hbm, base_ref, sems.at[1]),
    ] + [
        pltpu.make_async_copy(
            grad_hbm.at[:, cut:end], grad_ref.at[:, cut:end], sems.at[2 + i]
        )
        for i, (cut, end) in enumerate(zip(cuts, cuts[1:], strict=False))
    ]
    loads.append(
        pltpu.make_async_copy(
            w_hbm.at[: head_ref.shape[0], : head_ref.shape[1]], head_ref, sems.at[1 + len(cuts)]
        )
    )
    for load in loads:
        load.start()
    stores = [
        pltpu.make_async_copy(x_ref, copies_hbm.at[i], copy_sems.at[i])
        for i in range(copies_hbm.shape[0])
    ]
    loads[1].wait()
    rows, f_local = grad_ref.shape
    shape = (rows, rows)
    diagonal = lax.broadcasted_iota(jnp.int32, shape, 0) == lax.broadcasted_iota(
        jnp.int32, shape, 1
    )
    base = jnp.where(diagonal, jnp.broadcast_to(base_ref[...], shape), 0)
    base = jnp.sum(base, axis=1, keepdims=True)
    col_first = lax.axis_index("col") * f_local
    offset = seed_ref[0] * jnp.int32(1013904223)
    loads[0].wait()
    for store in stores:
        store.start()
    for out_ref, load, cut, end in zip(out_refs, loads[2:-1], cuts, cuts[1:], strict=False):
        load.wait()
        width = largest_block(end - cut, 256)
        for start in range(cut, end, width):
            columns = lax.broadcasted_iota(jnp.int32, (rows, width), 1)
            counter = base + (columns + (col_first + start))
            mixed = counter * jnp.int32(747796405) + offset
            mixed = mixed ^ (mixed >> 15)
            mixed = mixed * jnp.int32(277803737)
            mixed = mixed ^ (mixed >> 16)
            level = (mixed & 255).astype(jnp.float32)
            grad = grad_ref[:, start : start + width].astype(jnp.float32)
            done = jnp.floor(grad * 4.0 + (level + 0.5) / 256.0) / 4.0
            pieces = [done[i : i + per_col] for i in range(0, rows, per_col)]
            pieces = [p for c in range(CORES) for p in pieces[c::CORES]]
            at = slice(start - cut, start - cut + width)
            out_ref[:, at] = jnp.concatenate(pieces).astype(out_ref.dtype)
    for store in stores:
        store.wait()
    loads[-1].wait()


def stochastic_round(
    grad, counter_base, round_seed, activations, up_weight, cuts, n_chip
):
    per_col, d_local = activations.shape
    rows = grad.shape[0]
    vmem = pl.BlockSpec(memory_space=pltpu.VMEM)
    hbm = pl.BlockSpec(memory_space=pltpu.HBM)
    *parts, copies, head = pl.pallas_call(
        functools.partial(round_kernel, per_col, cuts),
        out_shape=[
            jax.ShapeDtypeStruct((rows, end - cut), jnp.bfloat16)
            for cut, end in zip(cuts, cuts[1:], strict=False)
        ]
        + [
            pltpu.HBM((n_chip, per_col, d_local), activations.dtype),
            jax.ShapeDtypeStruct((project_block(d_local), cuts[1]), up_weight.dtype),
        ],
        in_specs=[pl.BlockSpec(memory_space=pltpu.SMEM)] + [hbm] * 4,
        out_specs=[vmem] * (len(cuts) - 1) + [hbm, vmem],
        scratch_shapes=[
            pltpu.VMEM((1, rows), jnp.int32),
            pltpu.VMEM(grad.shape, grad.dtype),
            pltpu.VMEM(activations.shape, activations.dtype),
            pltpu.SemaphoreType.DMA((2 + len(cuts),)),
            pltpu.SemaphoreType.DMA((n_chip,)),
        ],
        name="quantize",
        cost_estimate=pl.CostEstimate(
            flops=16 * grad.size, bytes_accessed=4 * grad.size, transcendentals=0
        ),
        compiler_params=pltpu.CompilerParams(vmem_limit_bytes=8 * MIB),
    )(round_seed, *in_hbm(counter_base[None, :], grad, activations, up_weight))
    return parts, copies, head


def in_hbm(*arrays):
    return [pltpu.with_memory_space_constraint(a, pltpu.HBM) for a in arrays]


def largest_block(length, most):
    return next(b for b in range(min(most, length), 0, -1) if length % b == 0)


def row_start(j, rows, size):
    owner = lax.rem(lax.axis_index("row") - j + rows, rows)
    return pl.multiple_of(owner * size, size)


def project_block(d_local):
    return largest_block(d_local, 512)


def project_kernel(n_row, first, final, d_from, f_from, next_at, block, *refs):
    q_refs, refs = refs[:n_row], list(refs[n_row:])
    sum_ref = None if first else refs.pop(0)
    head_ref, w_hbm = refs.pop(0), refs.pop(0)
    out_refs = [refs.pop(0) for _ in range(CORES if final else 1)]
    ahead_ref = None if next_at is None else refs.pop(0)
    w_ref, sems = refs.pop(0), refs.pop(0)
    head = head_ref.shape[0] // block
    tr, f_len = q_refs[0].shape
    half = tr // CORES
    core = lax.rem(lax.axis_index("col"), CORES)
    steps = out_refs[0].shape[1 if final else 0] // block

    def rows_of(step, start=0):
        return pl.ds(pl.multiple_of(step * block + start, block), block)

    def fetch(step):
        source = w_hbm.at[rows_of(step, d_from), pl.ds(f_from, f_len)]
        return pltpu.make_async_copy(source, w_ref.at[rows_of(step - head), :], sems.at[step])

    def multiply(step, weight_ref, weight_step):
        at_d = rows_of(step)
        part = lax.dot_general(
            weight_ref[rows_of(weight_step), :],
            jnp.concatenate([q_ref[...] for q_ref in q_refs], axis=0),
            (((1,), (1,)), ((), ())),
            preferred_element_type=jnp.float32,
        )
        if sum_ref is not None:
            part = part + sum_ref[rows_of(step, d_from), :]
        if not final:
            out_refs[0][at_d, :] = part
            return
        turned_ref = refs[0]
        turned_ref[...] = part.astype(jnp.bfloat16).T
        for j in range(n_row):
            at = pl.ds(row_start(j, n_row, half), half)
            for out_ref, c in zip(out_refs, (core, 1 - core), strict=True):
                source = pl.multiple_of(j * tr + c * half, half)
                out_ref[at, at_d] = turned_ref[pl.ds(source, half), :]

    for step in range(head, steps):
        fetch(step).start()
    if ahead_ref is not None:
        d_next, f_next = next_at
        n_d, n_f = ahead_ref.shape
        source = w_hbm.at[d_next : d_next + n_d, f_next : f_next + n_f]
        ahead = pltpu.make_async_copy(source, ahead_ref, sems.at[steps])
        ahead.start()

    @pl.loop(0, head)
    def _(step):
        multiply(step, head_ref, step)

    if head < steps:

        @pl.loop(head, steps)
        def _(step):
            fetch(step).wait()
            multiply(step, w_ref, step - head)

    if ahead_ref is not None:
        ahead.wait()


def project(q_parts, up_weight, total, head, d_cut, f_from, final, following=None):
    n_row = len(q_parts)
    tr, f_len = q_parts[0].shape
    tokens = tr * n_row
    d_from, d_to = d_cut
    size = d_to - d_from
    block = project_block(up_weight.shape[0])
    steps = size // block
    vmem = pl.BlockSpec(memory_space=pltpu.VMEM)
    scratch = [
        pltpu.VMEM((max(size - head.shape[0], block), f_len), up_weight.dtype),
        pltpu.SemaphoreType.DMA((steps + 1,)),
    ]
    if final:
        scratch.append(pltpu.VMEM((tokens, block), jnp.bfloat16))
        out = [jax.ShapeDtypeStruct((tokens // CORES, size), jnp.bfloat16)] * CORES
    else:
        out = [jax.ShapeDtypeStruct((size, tokens), jnp.float32)]
    next_at = None
    if following is not None:
        next_at = tuple(start for start, _ in following)
        shape = tuple(end - start for start, end in following)
        out.append(jax.ShapeDtypeStruct(shape, up_weight.dtype))
    before = [] if total is None else [total]
    return pl.pallas_call(
        functools.partial(
            project_kernel, n_row, total is None, final, d_from, f_from, next_at, block
        ),
        out_shape=out,
        in_specs=[vmem] * (n_row + len(before) + 1) + [pl.BlockSpec(memory_space=pltpu.HBM)],
        out_specs=[vmem] * len(out),
        scratch_shapes=scratch,
        name="project",
        cost_estimate=pl.CostEstimate(
            flops=2 * tokens * size * f_len,
            bytes_accessed=2 * size * f_len,
            transcendentals=0,
        ),
        compiler_params=pltpu.CompilerParams(vmem_limit_bytes=VMEM_PROJECT * MIB),
    )(*q_parts, *before, head, *in_hbm(up_weight))


VMEM_PROJECT = 28
VMEM_WGRAD = 32


def pair_kernel(at, keep_ref, taken_ref, *refs):
    out_hbm, sum_ref, sem = refs[-3:]
    total = keep_ref[...].astype(jnp.float32) + taken_ref[...].astype(jnp.float32)
    sum_ref[...] = total.astype(sum_ref.dtype)
    store = pltpu.make_async_copy(sum_ref, out_hbm.at[:, pl.ds(at, keep_ref.shape[1])], sem)
    store.start()
    store.wait()


def pair_sum(keep, taken, at, d_local, into=None):
    vmem, hbm = (pl.BlockSpec(memory_space=m) for m in (pltpu.VMEM, pltpu.HBM))
    whole = [] if into is None else [into]
    return pl.pallas_call(
        functools.partial(pair_kernel, at),
        out_shape=jax.ShapeDtypeStruct((keep.shape[0], d_local), keep.dtype),
        in_specs=[vmem] * 2 + [hbm] * len(whole),
        out_specs=hbm,
        input_output_aliases={2: 0} if whole else {},
        scratch_shapes=[pltpu.VMEM(keep.shape, keep.dtype), pltpu.SemaphoreType.DMA(())],
        name="pairsum",
        cost_estimate=pl.CostEstimate(
            flops=keep.size, bytes_accessed=6 * keep.size, transcendentals=0
        ),
        compiler_params=pltpu.CompilerParams(vmem_limit_bytes=8 * MIB),
    )(keep, taken, *whole)


def wgrad_kernel(n_row, n_cut, scaling, *refs):
    q_refs, refs = refs[: n_row * n_cut], refs[n_row * n_cut :]
    mine_ref, other_ref, out_hbm, x_ref, q_ref, held, sems = refs
    tr = q_refs[0].shape[0]
    half = tr // CORES
    slots, block, _ = held.shape
    core = lax.rem(lax.axis_index("col"), CORES)
    for c in range(CORES):

        @pl.when(core == c)
        def _():
            for j in range(n_row):
                at = pl.ds(row_start(j, n_row, half), half)
                for k in range(CORES):
                    source = mine_ref if k == c else other_ref
                    to = j * tr + k * half
                    x_ref[to : to + half, :] = source[at, :]

    for j in range(n_row):
        start = 0
        for i in range(n_cut):
            part = q_refs[i * n_row + j]
            end = start + part.shape[1]
            q_ref[j * tr : (j + 1) * tr, start:end] = part[...]
            start = end

    f_local = out_hbm.shape[1]
    cuts = (0, f_local // (2 * LANES) * LANES, f_local)
    sides = [slice(*side) for side in zip(cuts, cuts[1:], strict=False)]

    def store(step, side):
        slot = lax.rem(step, slots)
        rows = pl.ds(pl.multiple_of(step * block, block), block)
        return pltpu.make_async_copy(
            held.at[slot, :, sides[side]], out_hbm.at[rows, sides[side]], sems.at[slot, side]
        )

    steps = out_hbm.shape[0] // block

    @pl.loop(0, steps)
    def _(step):
        rows = pl.ds(pl.multiple_of(step * block, block), block)
        for side in range(len(sides)):

            @pl.when(step >= slots)
            def _():
                store(step - slots, side).wait()

            held[lax.rem(step, slots), :, sides[side]] = scaling * lax.dot_general(
                x_ref[:, rows],
                q_ref[:, sides[side]],
                (((0,), (0,)), ((), ())),
                preferred_element_type=jnp.float32,
            )
            store(step, side).start()

    for step in range(max(steps - slots, 0), steps):
        for side in range(len(sides)):
            store(step, side).wait()


def wgrad(q_cuts, x_mine, x_other, scaling):
    n_cut, n_row = len(q_cuts), len(q_cuts[0])
    tr = q_cuts[0][0].shape[0]
    f_local = sum(parts[0].shape[1] for parts in q_cuts)
    tokens, d_local = tr * n_row, x_mine.shape[1]
    block = largest_block(d_local, 256)
    slots = min(3, d_local // block)
    vmem = pl.BlockSpec(memory_space=pltpu.VMEM)
    return pl.pallas_call(
        functools.partial(wgrad_kernel, n_row, n_cut, scaling),
        out_shape=jax.ShapeDtypeStruct((d_local, f_local), jnp.float32),
        in_specs=[vmem] * (n_row * n_cut + 2),
        out_specs=pl.BlockSpec(memory_space=pltpu.HBM),
        scratch_shapes=[
            pltpu.VMEM((tokens, d_local), jnp.bfloat16),
            pltpu.VMEM((tokens, f_local), jnp.bfloat16),
            pltpu.VMEM((slots, block, f_local), jnp.float32),
            pltpu.SemaphoreType.DMA((slots, 2)),
        ],
        name="wgrad",
        cost_estimate=pl.CostEstimate(
            flops=2 * tokens * d_local * f_local,
            bytes_accessed=4 * d_local * f_local,
            transcendentals=0,
        ),
        compiler_params=pltpu.CompilerParams(vmem_limit_bytes=VMEM_WGRAD * MIB),
    )(*[part for parts in q_cuts for part in parts], x_mine, x_other)


def shards(activations, up_weight, out_grad, round_seed, counter_base):
    n_row, n_col = lax.axis_size("row"), lax.axis_size("col")
    n_chip = n_col // CORES
    assert n_col % (CORES * n_row) == 0
    per_col, d_local = activations.shape
    tokens = per_col * n_col
    chips = [[chip * CORES + c for chip in range(n_chip)] for c in range(CORES)]
    swap = [(i, i ^ 1) for i in range(n_col)]

    f_local = out_grad.shape[1]
    middle = -(-f_local // (2 * LANES)) * LANES
    cuts = (0, middle, f_local)
    block = project_block(d_local)
    steps = d_local // block
    d_head, d_cut = block * max(1, steps // 4), block * (3 * steps // 4)
    shifts = [[(i, (i + j) % n_row) for i in range(n_row)] for j in range(1, n_row)]
    owns, copies, head = stochastic_round(
        out_grad, counter_base, round_seed, activations, up_weight, cuts, n_chip
    )
    q_a = [owns[0]] + [lax.ppermute(owns[0], "row", shift) for shift in shifts]
    q_b = [owns[1]] + [lax.ppermute(owns[1], "row", shift) for shift in shifts]
    x_mine = lax.all_to_all(copies, "col", 0, 0, axis_index_groups=chips)
    x_mine = x_mine.reshape(n_chip * per_col, d_local)
    x_other = lax.ppermute(x_mine, "col", swap)
    total, head = project(
        q_a, up_weight, None, head, (0, d_local), 0, False, ((0, d_head), (middle, f_local))
    )
    keep_a, give_a, head = project(
        q_b, up_weight, total, head, (0, d_cut), middle, True, ((d_cut, d_local), (middle, f_local))
    )
    keep_b, give_b = project(q_b, up_weight, total, head, (d_cut, d_local), middle, True)
    taken_a = lax.ppermute(give_a, "col", swap)
    taken_b = lax.ppermute(give_b, "col", swap)
    pair = pair_sum(keep_a, taken_a, 0, d_local)
    pair = pair_sum(keep_b, taken_b, d_cut, d_local, pair)
    pair = pair.reshape(n_chip, per_col, d_local)
    shares = lax.all_to_all(pair, "col", 0, 0, axis_index_groups=chips)
    weight_grad = wgrad((q_a, q_b), x_mine, x_other, tokens ** (-0.5))
    input_grad = jnp.sum(shares.astype(jnp.float32), axis=0)
    return weight_grad, input_grad.astype(jnp.bfloat16)


def solution(mesh):
    placed = (P("col", "row"), P("row", "col"), P("row", "col"), P(), P("row"))
    return jax.shard_map(
        shards,
        mesh=mesh,
        in_specs=placed,
        out_specs=(P("row", "col"), P("col", "row")),
        check_vma=False,
    )
```

profile of v0, /device:TPU:0, one launch (start us, length us, event | category | flops | bytes accessed | tf_op | source)
XLA Modules:
  0.0 59.2 jit_solution(5730390233708005709)
XLA Ops:
  1.3 1.9 %quantize.1 = (bf16[64,1792]{1,0:T(8,128)(2,1)S(1)}, bf16[64,1536]{1,0:T(8,128)(2,1)S(1)}, bf16[8,8,4096]{2,1,0:T(8,128)(2,1)}, bf16[512,1792]{1,0:T(8,128)(2,1)S(1)}) custom-call(s32[1]{0:T(128)S(6)} %copy.9.seed_ref, s32[1,64]{1,0:T(1,128)} %bitcast.5, bf16[64,3328]{1,0:T(8,128)(2,1)} %grad_hbm.1, bf16[8,4096]{1,0:T(8,128)(2,1)} %x_hbm.1, ...), custom_call_target="tpu_custom_call" | custom-call | flops 3407872 | bytes 851968 | tf_op jit(solution)/shard_map/quantize/pallas_call | solution.py:82
  3.2 7.3 %all-to-all-start = ((bf16[8,8,4096]{2,1,0:T(8,128)(2,1)}), bf16[8,8,4096]{2,1,0:T(8,128)(2,1)S(1)}, u32[]{:S(2)}, u32[]{:S(2)}) async-start(bf16[8,8,4096]{2,1,0:T(8,128)(2,1)} %get-tuple-element.15), calls=%async_computation | async-start | bytes 1048576 | tf_op jit(solution)/shard_map/all_to_all | solution.py:376
  10.5 1.5 %collective-permute-start = (bf16[64,1792]{1,0:T(8,128)(2,1)S(1)}, bf16[64,1792]{1,0:T(8,128)(2,1)S(1)}, u32[]{:S(2)}, u32[]{:S(2)}) collective-permute-start(bf16[64,1792]{1,0:T(8,128)(2,1)S(1)} %get-tuple-element.13.refs_0_), channel_id=1, source_target_pairs={{0,16},{16,0},{1,17},{17,1},{2,18},{18,2},{3,19},{19,3},{4,20},{20... | collective-permute-start | bytes 688136 | tf_op jit(solution)/shard_map/ppermute | solution.py:374
  12.0 0.5 collective-permute-start.1
  12.5 6.4 %collective-permute-done.refs_1_ = bf16[64,1792]{1,0:T(8,128)(2,1)S(1)} collective-permute-done((bf16[64,1792]{1,0:T(8,128)(2,1)S(1)}, bf16[64,1792]{1,0:T(8,128)(2,1)S(1)}, u32[]{:S(2)}, u32[]{:S(2)}) %collective-permute-start) | collective-permute-done | bytes 229408 | tf_op jit(solution)/shard_map/ppermute | solution.py:374
  19.0 6.1 %project.3 = (f32[4096,128]{1,0:T(8,128)S(1)}, bf16[1024,1536]{1,0:T(8,128)(2,1)S(1)}) custom-call(bf16[64,1792]{1,0:T(8,128)(2,1)S(1)} %get-tuple-element.13.refs_0_, bf16[64,1792]{1,0:T(8,128)(2,1)S(1)} %collective-permute-done.refs_1_, bf16[512,1792]{1,0:T(8,128)(2,1)S(1)} %get-tuple-element.16.refs_2_, bf16[4096,3328]{1,0:T(8,128)(2,1)} %refs_4_.3), custom_call_target="tpu_custom_call" | custom-call | flops 1879048192 | bytes 14680064 | tf_op jit(solution)/shard_map/project/pallas_call | solution.py:216
  25.0 0.0 collective-permute-done.1.refs_3_.refs_1_
  25.0 4.0 %project.4 = (bf16[64,3072]{1,0:T(8,128)(2,1)S(1)}, bf16[64,3072]{1,0:T(8,128)(2,1)S(1)}, bf16[1024,1536]{1,0:T(8,128)(2,1)S(1)}) custom-call(bf16[64,1536]{1,0:T(8,128)(2,1)S(1)} %get-tuple-element.14.refs_2_.refs_0_, bf16[64,1536]{1,0:T(8,128)(2,1)S(1)} %collective-permute-done.1.refs_3_.refs_1_, f32[4096,128]{1,0:T(8,128)S(1)} %get-tuple-element.17.refs_2_, ...), custom_call_target="tpu_custom_call" | custom-call | flops 1207959552 | bytes 9437184 | tf_op jit(solution)/shard_map/project/pallas_call | solution.py:216
  29.1 0.1 collective-permute-start.4
  29.2 1.3 %project.5 = (bf16[64,1024]{1,0:T(8,128)(2,1)S(1)}, bf16[64,1024]{1,0:T(8,128)(2,1)S(1)}) custom-call(bf16[64,1536]{1,0:T(8,128)(2,1)S(1)} %get-tuple-element.14.refs_2_.refs_0_, bf16[64,1536]{1,0:T(8,128)(2,1)S(1)} %collective-permute-done.1.refs_3_.refs_1_, f32[4096,128]{1,0:T(8,128)S(1)} %get-tuple-element.17.refs_2_, ...), custom_call_target="tpu_custom_call" | custom-call | flops 402653184 | bytes 3145728 | tf_op jit(solution)/shard_map/project/pallas_call | solution.py:216
  30.5 0.6 collective-permute-start.3
  31.0 0.0 collective-permute-done.4.taken_ref
  31.1 0.9 %pairsum.2.refs_0_ = bf16[64,4096]{1,0:T(8,128)(2,1)} custom-call(bf16[64,3072]{1,0:T(8,128)(2,1)S(1)} %get-tuple-element.22.keep_ref, bf16[64,3072]{1,0:T(8,128)(2,1)S(1)} %collective-permute-done.4.taken_ref), custom_call_target="tpu_custom_call" | custom-call | flops 196608 | bytes 1179648 | tf_op jit(solution)/shard_map/pairsum/pallas_call | solution.py:250
  31.9 0.1 collective-permute-done.3.taken_ref
  32.0 0.7 %pairsum.3 = bf16[64,4096]{1,0:T(8,128)(2,1)} custom-call(bf16[64,1024]{1,0:T(8,128)(2,1)S(1)} %get-tuple-element.20.keep_ref, bf16[64,1024]{1,0:T(8,128)(2,1)S(1)} %collective-permute-done.3.taken_ref, bf16[64,4096]{1,0:T(8,128)(2,1)} %pairsum.2.refs_0_), custom_call_target="tpu_custom_call", output_to_operand_aliasing={{}: (2, {})} | custom-call | flops 65536 | bytes 393216 | tf_op jit(solution)/shard_map/pairsum/pallas_call | solution.py:250
  32.8 0.0 all-to-all-done
  32.8 6.0 %all-to-all-start.1 = ((bf16[8,8,4096]{2,1,0:T(8,128)(2,1)}), bf16[8,8,4096]{2,1,0:T(8,128)(2,1)S(1)}, u32[]{:S(2)}, u32[]{:S(2)}) async-start(bf16[8,8,4096]{2,1,0:T(8,128)(2,1)} %bitcast.2), calls=%async_computation.1 | async-start | bytes 1048576 | tf_op jit(solution)/shard_map/all_to_all | solution.py:391
  38.8 0.1 collective-permute-start.2
  38.9 1.8 %collective-permute-done.2.refs_5_ = bf16[64,4096]{1,0:T(8,128)(2,1)S(1)} collective-permute-done((bf16[64,4096]{1,0:T(8,128)(2,1)S(1)}, bf16[64,4096]{1,0:T(8,128)(2,1)S(1)}, u32[]{:S(2)}, u32[]{:S(2)}) %collective-permute-start.2) | collective-permute-done | bytes 524320 | tf_op jit(solution)/shard_map/ppermute | solution.py:378
  40.7 17.8 %wgrad.1 = f32[4096,3328]{1,0:T(8,128)} custom-call(bf16[64,1792]{1,0:T(8,128)(2,1)S(1)} %get-tuple-element.13.refs_0_, bf16[64,1792]{1,0:T(8,128)(2,1)S(1)} %collective-permute-done.refs_1_, bf16[64,1536]{1,0:T(8,128)(2,1)S(1)} %get-tuple-element.14.refs_2_.refs_0_, bf16[64,1536]{1,0:T(8,128)(2,1)S(1)} %collective-permute-done.1.refs_3_.refs_1_, ...), custom_call_target="tpu_custom_call" | custom-call | flops 3489660928 | bytes 54525952 | tf_op jit(solution)/shard_map/wgrad/pallas_call | solution.py:334
  58.5 0.0 all-to-all-done.1
  58.5 0.7 %reduce_sum.12 = bf16[8,4096]{1,0:T(8,128)(2,1)} reduce(bf16[8,8,4096]{2,1,0:T(8,128)(2,1)S(1)} %all-to-all-done.1, bf16[]{:T(256)} %constant.2.clone.1), dimensions={0}, to_apply=%region_0.0 | reduce | flops 229376 | bytes 589826 | tf_op jit(solution)/shard_map/reduce_sum | solution.py:393
Async XLA Ops:
  3.2 29.6 %all-to-all-start = ((bf16[8,8,4096]{2,1,0:T(8,128)(2,1)}), bf16[8,8,4096]{2,1,0:T(8,128)(2,1)S(1)}, u32[]{:S(2)}, u32[]{:S(2)}) async-start(bf16[8,8,4096]{2,1,0:T(8,128)(2,1)} %get-tuple-element.15), calls=%async_computation | async-start | bytes 1048576 | tf_op jit(solution)/shard_map/all_to_all | solution.py:376
  10.5 8.5 %collective-permute-start = (bf16[64,1792]{1,0:T(8,128)(2,1)S(1)}, bf16[64,1792]{1,0:T(8,128)(2,1)S(1)}, u32[]{:S(2)}, u32[]{:S(2)}) collective-permute-start(bf16[64,1792]{1,0:T(8,128)(2,1)S(1)} %get-tuple-element.13.refs_0_), channel_id=1, source_target_pairs={{0,16},{16,0},{1,17},{17,1},{2,18},{18,2},{3,19},{19,3},{4,20},{20... | collective-permute-start | bytes 688136 | tf_op jit(solution)/shard_map/ppermute | solution.py:374
  12.0 13.0 %collective-permute-start.1 = (bf16[64,1536]{1,0:T(8,128)(2,1)S(1)}, bf16[64,1536]{1,0:T(8,128)(2,1)S(1)}, u32[]{:S(2)}, u32[]{:S(2)}) collective-permute-start(bf16[64,1536]{1,0:T(8,128)(2,1)S(1)} %get-tuple-element.14.refs_2_.refs_0_), channel_id=1, source_target_pairs={{0,16},{16,0},{1,17},{17,1},{2,18},{18,2},{3,19},{19,3},{4,20},{20... | collective-permute-start | bytes 589832 | tf_op jit(solution)/shard_map/ppermute | solution.py:375
  29.1 2.0 %collective-permute-start.4 = (bf16[64,3072]{1,0:T(8,128)(2,1)S(1)}, bf16[64,3072]{1,0:T(8,128)(2,1)S(1)}, u32[]{:S(2)}, u32[]{:S(2)}) collective-permute-start(bf16[64,3072]{1,0:T(8,128)(2,1)S(1)} %get-tuple-element.23), channel_id=1, source_target_pairs={{0,1},{1,0},{2,3},{3,2},{4,5},{5,4},{6,7},{7,6},{8,9},{9,8},{10,11... | collective-permute-start | bytes 1179656 | tf_op jit(solution)/shard_map/ppermute | solution.py:386
  30.5 1.5 %collective-permute-start.3 = (bf16[64,1024]{1,0:T(8,128)(2,1)S(1)}, bf16[64,1024]{1,0:T(8,128)(2,1)S(1)}, u32[]{:S(2)}, u32[]{:S(2)}) collective-permute-start(bf16[64,1024]{1,0:T(8,128)(2,1)S(1)} %get-tuple-element.21), channel_id=1, source_target_pairs={{0,1},{1,0},{2,3},{3,2},{4,5},{5,4},{6,7},{7,6},{8,9},{9,8},{10,11... | collective-permute-start | bytes 393224 | tf_op jit(solution)/shard_map/ppermute | solution.py:387
  32.8 25.7 %all-to-all-start.1 = ((bf16[8,8,4096]{2,1,0:T(8,128)(2,1)}), bf16[8,8,4096]{2,1,0:T(8,128)(2,1)S(1)}, u32[]{:S(2)}, u32[]{:S(2)}) async-start(bf16[8,8,4096]{2,1,0:T(8,128)(2,1)} %bitcast.2), calls=%async_computation.1 | async-start | bytes 1048576 | tf_op jit(solution)/shard_map/all_to_all | solution.py:391
  38.8 1.9 %collective-permute-start.2 = (bf16[64,4096]{1,0:T(8,128)(2,1)S(1)}, bf16[64,4096]{1,0:T(8,128)(2,1)S(1)}, u32[]{:S(2)}, u32[]{:S(2)}) collective-permute-start(bf16[64,4096]{1,0:T(8,128)(2,1)S(1)} %bitcast.3), channel_id=1, source_target_pairs={{0,1},{1,0},{2,3},{3,2},{4,5},{5,4},{6,7},{7,6},{8,9},{9,8},{10,11... | collective-permute-start | bytes 1572872 | tf_op jit(solution)/shard_map/ppermute | solution.py:378
where the time goes:
time: 59.6 us; the launch traced here: 59.2 us
  Pallas kernels  32.7 us (55%)
  starting transfers between devices  16.1 us (27%)
  waiting for transfers between devices  8.38 us (14%)
  between operations  1.37 us (2%)
  other arithmetic  0.7 us (1%)
    pallas_call x1, Pallas kernels, wgrad(): pl.pallas_call(functools.partial(wgrad_kernel, n_row, n_cut, scaling), ou...  17.8 us
    pallas_call x3, Pallas kernels, project(): pl.pallas_call(functools.partial(project_kernel, n_row, total is None, fi...  11.4 us
    all_to_all x1, starting transfers between devices, shards(): x_mine = lax.all_to_all(copies, 'col', 0, 0, axis_index_groups=chips)  7.32 us
    ppermute x1, waiting for transfers between devices, shards(): q_a = [owns[0]] + [lax.ppermute(owns[0], 'row', shift) for shift in shifts]  6.45 us
    all_to_all x1, starting transfers between devices, shards(): shares = lax.all_to_all(pair, 'col', 0, 0, axis_index_groups=chips)  6.01 us
    pallas_call x1, Pallas kernels, stochastic_round(): pl.pallas_call(functools.partial(round_kernel, per_col, cuts), out_shape=...  1.89 us
    ppermute x1, waiting for transfers between devices, shards(): x_other = lax.ppermute(x_mine, 'col', swap)  1.83 us
    pallas_call x2, Pallas kernels, pair_sum(): pl.pallas_call(functools.partial(pair_kernel, at), out_shape=jax.ShapeDty...  1.62 us
  transfers between devices with their start and end apart: 7, of which 3 were waited for; matrix products, arithmetic and copies ran while one was open for 0% of the time, Pallas kernels for 52%

commit v1 on v0

--- a/solution.py
+++ b/solution.py
@@ -269,17 +269,6 @@
     half = tr // CORES
     slots, block, _ = held.shape
     core = lax.rem(lax.axis_index("col"), CORES)
-    for c in range(CORES):
-
-        @pl.when(core == c)
-        def _():
-            for j in range(n_row):
-                at = pl.ds(row_start(j, n_row, half), half)
-                for k in range(CORES):
-                    source = mine_ref if k == c else other_ref
-                    to = j * tr + k * half
-                    x_ref[to : to + half, :] = source[at, :]
-
     for j in range(n_row):
         start = 0
         for i in range(n_cut):
@@ -289,7 +278,8 @@
             start = end
 
     f_local = out_hbm.shape[1]
-    cuts = (0, f_local // (2 * LANES) * LANES, f_local)
+    count = sems.shape[1]
+    cuts = [i * (f_local // LANES) // count * LANES for i in range(count)] + [f_local]
     sides = [slice(*side) for side in zip(cuts, cuts[1:], strict=False)]
 
     def store(step, side):
@@ -304,6 +294,17 @@
     @pl.loop(0, steps)
     def _(step):
         rows = pl.ds(pl.multiple_of(step * block, block), block)
+        for c in range(CORES):
+
+            @pl.when(core == c)
+            def _():
+                for j in range(n_row):
+                    at = pl.ds(row_start(j, n_row, half), half)
+                    for k in range(CORES):
+                        source = mine_ref if k == c else other_ref
+                        to = j * tr + k * half
+                        x_ref[to : to + half, :] = source[at, rows]
+
         for side in range(len(sides)):
 
             @pl.when(step >= slots)
@@ -311,7 +312,7 @@
                 store(step - slots, side).wait()
 
             held[lax.rem(step, slots), :, sides[side]] = scaling * lax.dot_general(
-                x_ref[:, rows],
+                x_ref[...],
                 q_ref[:, sides[side]],
                 (((0,), (0,)), ((), ())),
                 preferred_element_type=jnp.float32,
@@ -337,7 +338,7 @@
         in_specs=[vmem] * (n_row * n_cut + 2),
         out_specs=pl.BlockSpec(memory_space=pltpu.HBM),
         scratch_shapes=[
-            pltpu.VMEM((tokens, d_local), jnp.bfloat16),
+            pltpu.VMEM((tokens, block), jnp.bfloat16),
             pltpu.VMEM((tokens, f_local), jnp.bfloat16),
             pltpu.VMEM((slots, block, f_local), jnp.float32),
             pltpu.SemaphoreType.DMA((slots, 2)),

time: 59.6 us -> 59.5 us (level)
  no operation moved by 1% of the time
where the time goes in v1:
time: 59.5 us; the launch traced here: 59.2 us
  Pallas kernels  32.7 us (55%)
  starting transfers between devices  16.1 us (27%)
  waiting for transfers between devices  8.38 us (14%)
  between operations  1.37 us (2%)
  other arithmetic  0.7 us (1%)
    pallas_call x1, Pallas kernels, wgrad(): pl.pallas_call(functools.partial(wgrad_kernel, n_row, n_cut, scaling), ou...  17.8 us
    pallas_call x3, Pallas kernels, project(): pl.pallas_call(functools.partial(project_kernel, n_row, total is None, fi...  11.4 us
    all_to_all x1, starting transfers between devices, shards(): x_mine = lax.all_to_all(copies, 'col', 0, 0, axis_index_groups=chips)  7.32 us
    ppermute x1, waiting for transfers between devices, shards(): q_a = [owns[0]] + [lax.ppermute(owns[0], 'row', shift) for shift in shifts]  6.45 us
    all_to_all x1, starting transfers between devices, shards(): shares = lax.all_to_all(pair, 'col', 0, 0, axis_index_groups=chips)  6.01 us
    pallas_call x1, Pallas kernels, stochastic_round(): pl.pallas_call(functools.partial(round_kernel, per_col, cuts), out_shape=...  1.89 us
    ppermute x1, waiting for transfers between devices, shards(): x_other = lax.ppermute(x_mine, 'col', swap)  1.83 us
    pallas_call x2, Pallas kernels, pair_sum(): pl.pallas_call(functools.partial(pair_kernel, at), out_shape=jax.ShapeDty...  1.62 us
  transfers between devices with their start and end apart: 7, of which 3 were waited for; matrix products, arithmetic and copies ran while one was open for 0% of the time, Pallas kernels for 52%

profile of v1, /device:TPU:0, one launch (start us, length us, event | category | flops | bytes accessed | tf_op | source)
XLA Modules:
  0.0 59.2 jit_solution(16644108087249622080)
XLA Ops:
  1.3 1.9 %quantize.1 = (bf16[64,1792]{1,0:T(8,128)(2,1)S(1)}, bf16[64,1536]{1,0:T(8,128)(2,1)S(1)}, bf16[8,8,4096]{2,1,0:T(8,128)(2,1)}, bf16[512,1792]{1,0:T(8,128)(2,1)S(1)}) custom-call(s32[1]{0:T(128)S(6)} %copy.9.seed_ref, s32[1,64]{1,0:T(1,128)} %bitcast.5, bf16[64,3328]{1,0:T(8,128)(2,1)} %grad_hbm.1, bf16[8,4096]{1,0:T(8,128)(2,1)} %x_hbm.1, ...), custom_call_target="tpu_custom_call" | custom-call | flops 3407872 | bytes 851968 | tf_op jit(solution)/shard_map/quantize/pallas_call | solution.py:82
  3.2 7.3 %all-to-all-start = ((bf16[8,8,4096]{2,1,0:T(8,128)(2,1)}), bf16[8,8,4096]{2,1,0:T(8,128)(2,1)S(1)}, u32[]{:S(2)}, u32[]{:S(2)}) async-start(bf16[8,8,4096]{2,1,0:T(8,128)(2,1)} %get-tuple-element.15), calls=%async_computation | async-start | bytes 1048576 | tf_op jit(solution)/shard_map/all_to_all | solution.py:377
  10.5 1.5 %collective-permute-start = (bf16[64,1792]{1,0:T(8,128)(2,1)S(1)}, bf16[64,1792]{1,0:T(8,128)(2,1)S(1)}, u32[]{:S(2)}, u32[]{:S(2)}) collective-permute-start(bf16[64,1792]{1,0:T(8,128)(2,1)S(1)} %get-tuple-element.13.refs_0_), channel_id=1, source_target_pairs={{0,16},{16,0},{1,17},{17,1},{2,18},{18,2},{3,19},{19,3},{4,20},{20... | collective-permute-start | bytes 688136 | tf_op jit(solution)/shard_map/ppermute | solution.py:375
  12.0 0.5 collective-permute-start.1
  12.5 6.4 %collective-permute-done.refs_1_ = bf16[64,1792]{1,0:T(8,128)(2,1)S(1)} collective-permute-done((bf16[64,1792]{1,0:T(8,128)(2,1)S(1)}, bf16[64,1792]{1,0:T(8,128)(2,1)S(1)}, u32[]{:S(2)}, u32[]{:S(2)}) %collective-permute-start) | collective-permute-done | bytes 229408 | tf_op jit(solution)/shard_map/ppermute | solution.py:375
  19.0 6.1 %project.3 = (f32[4096,128]{1,0:T(8,128)S(1)}, bf16[1024,1536]{1,0:T(8,128)(2,1)S(1)}) custom-call(bf16[64,1792]{1,0:T(8,128)(2,1)S(1)} %get-tuple-element.13.refs_0_, bf16[64,1792]{1,0:T(8,128)(2,1)S(1)} %collective-permute-done.refs_1_, bf16[512,1792]{1,0:T(8,128)(2,1)S(1)} %get-tuple-element.16.refs_2_, bf16[4096,3328]{1,0:T(8,128)(2,1)} %refs_4_.3), custom_call_target="tpu_custom_call" | custom-call | flops 1879048192 | bytes 14680064 | tf_op jit(solution)/shard_map/project/pallas_call | solution.py:216
  25.0 0.0 collective-permute-done.1.refs_3_.refs_1_
  25.0 4.0 %project.4 = (bf16[64,3072]{1,0:T(8,128)(2,1)S(1)}, bf16[64,3072]{1,0:T(8,128)(2,1)S(1)}, bf16[1024,1536]{1,0:T(8,128)(2,1)S(1)}) custom-call(bf16[64,1536]{1,0:T(8,128)(2,1)S(1)} %get-tuple-element.14.refs_2_.refs_0_, bf16[64,1536]{1,0:T(8,128)(2,1)S(1)} %collective-permute-done.1.refs_3_.refs_1_, f32[4096,128]{1,0:T(8,128)S(1)} %get-tuple-element.17.refs_2_, ...), custom_call_target="tpu_custom_call" | custom-call | flops 1207959552 | bytes 9437184 | tf_op jit(solution)/shard_map/project/pallas_call | solution.py:216
  29.1 0.1 collective-permute-start.4
  29.2 1.3 %project.5 = (bf16[64,1024]{1,0:T(8,128)(2,1)S(1)}, bf16[64,1024]{1,0:T(8,128)(2,1)S(1)}) custom-call(bf16[64,1536]{1,0:T(8,128)(2,1)S(1)} %get-tuple-element.14.refs_2_.refs_0_, bf16[64,1536]{1,0:T(8,128)(2,1)S(1)} %collective-permute-done.1.refs_3_.refs_1_, f32[4096,128]{1,0:T(8,128)S(1)} %get-tuple-element.17.refs_2_, ...), custom_call_target="tpu_custom_call" | custom-call | flops 402653184 | bytes 3145728 | tf_op jit(solution)/shard_map/project/pallas_call | solution.py:216
  30.5 0.6 collective-permute-start.3
  31.0 0.0 collective-permute-done.4.taken_ref
  31.1 0.9 %pairsum.2.refs_0_ = bf16[64,4096]{1,0:T(8,128)(2,1)} custom-call(bf16[64,3072]{1,0:T(8,128)(2,1)S(1)} %get-tuple-element.22.keep_ref, bf16[64,3072]{1,0:T(8,128)(2,1)S(1)} %collective-permute-done.4.taken_ref), custom_call_target="tpu_custom_call" | custom-call | flops 196608 | bytes 1179648 | tf_op jit(solution)/shard_map/pairsum/pallas_call | solution.py:250
  31.9 0.1 collective-permute-done.3.taken_ref
  32.0 0.7 %pairsum.3 = bf16[64,4096]{1,0:T(8,128)(2,1)} custom-call(bf16[64,1024]{1,0:T(8,128)(2,1)S(1)} %get-tuple-element.20.keep_ref, bf16[64,1024]{1,0:T(8,128)(2,1)S(1)} %collective-permute-done.3.taken_ref, bf16[64,4096]{1,0:T(8,128)(2,1)} %pairsum.2.refs_0_), custom_call_target="tpu_custom_call", output_to_operand_aliasing={{}: (2, {})} | custom-call | flops 65536 | bytes 393216 | tf_op jit(solution)/shard_map/pairsum/pallas_call | solution.py:250
  32.8 0.0 all-to-all-done
  32.8 6.0 %all-to-all-start.1 = ((bf16[8,8,4096]{2,1,0:T(8,128)(2,1)}), bf16[8,8,4096]{2,1,0:T(8,128)(2,1)S(1)}, u32[]{:S(2)}, u32[]{:S(2)}) async-start(bf16[8,8,4096]{2,1,0:T(8,128)(2,1)} %bitcast.2), calls=%async_computation.1 | async-start | bytes 1048576 | tf_op jit(solution)/shard_map/all_to_all | solution.py:392
  38.8 0.1 collective-permute-start.2
  38.9 1.8 %collective-permute-done.2.refs_5_ = bf16[64,4096]{1,0:T(8,128)(2,1)S(1)} collective-permute-done((bf16[64,4096]{1,0:T(8,128)(2,1)S(1)}, bf16[64,4096]{1,0:T(8,128)(2,1)S(1)}, u32[]{:S(2)}, u32[]{:S(2)}) %collective-permute-start.2) | collective-permute-done | bytes 524320 | tf_op jit(solution)/shard_map/ppermute | solution.py:379
  40.7 17.8 %wgrad.1 = f32[4096,3328]{1,0:T(8,128)} custom-call(bf16[64,1792]{1,0:T(8,128)(2,1)S(1)} %get-tuple-element.13.refs_0_, bf16[64,1792]{1,0:T(8,128)(2,1)S(1)} %collective-permute-done.refs_1_, bf16[64,1536]{1,0:T(8,128)(2,1)S(1)} %get-tuple-element.14.refs_2_.refs_0_, bf16[64,1536]{1,0:T(8,128)(2,1)S(1)} %collective-permute-done.1.refs_3_.refs_1_, ...), custom_call_target="tpu_custom_call" | custom-call | flops 3489660928 | bytes 54525952 | tf_op jit(solution)/shard_map/wgrad/pallas_call | solution.py:335
  58.5 0.0 all-to-all-done.1
  58.5 0.7 %reduce_sum.12 = bf16[8,4096]{1,0:T(8,128)(2,1)} reduce(bf16[8,8,4096]{2,1,0:T(8,128)(2,1)S(1)} %all-to-all-done.1, bf16[]{:T(256)} %constant.2.clone.1), dimensions={0}, to_apply=%region_0.0 | reduce | flops 229376 | bytes 589826 | tf_op jit(solution)/shard_map/reduce_sum | solution.py:394
Async XLA Ops:
  3.2 29.6 %all-to-all-start = ((bf16[8,8,4096]{2,1,0:T(8,128)(2,1)}), bf16[8,8,4096]{2,1,0:T(8,128)(2,1)S(1)}, u32[]{:S(2)}, u32[]{:S(2)}) async-start(bf16[8,8,4096]{2,1,0:T(8,128)(2,1)} %get-tuple-element.15), calls=%async_computation | async-start | bytes 1048576 | tf_op jit(solution)/shard_map/all_to_all | solution.py:377
  10.5 8.5 %collective-permute-start = (bf16[64,1792]{1,0:T(8,128)(2,1)S(1)}, bf16[64,1792]{1,0:T(8,128)(2,1)S(1)}, u32[]{:S(2)}, u32[]{:S(2)}) collective-permute-start(bf16[64,1792]{1,0:T(8,128)(2,1)S(1)} %get-tuple-element.13.refs_0_), channel_id=1, source_target_pairs={{0,16},{16,0},{1,17},{17,1},{2,18},{18,2},{3,19},{19,3},{4,20},{20... | collective-permute-start | bytes 688136 | tf_op jit(solution)/shard_map/ppermute | solution.py:375
  12.0 13.0 %collective-permute-start.1 = (bf16[64,1536]{1,0:T(8,128)(2,1)S(1)}, bf16[64,1536]{1,0:T(8,128)(2,1)S(1)}, u32[]{:S(2)}, u32[]{:S(2)}) collective-permute-start(bf16[64,1536]{1,0:T(8,128)(2,1)S(1)} %get-tuple-element.14.refs_2_.refs_0_), channel_id=1, source_target_pairs={{0,16},{16,0},{1,17},{17,1},{2,18},{18,2},{3,19},{19,3},{4,20},{20... | collective-permute-start | bytes 589832 | tf_op jit(solution)/shard_map/ppermute | solution.py:376
  29.1 2.0 %collective-permute-start.4 = (bf16[64,3072]{1,0:T(8,128)(2,1)S(1)}, bf16[64,3072]{1,0:T(8,128)(2,1)S(1)}, u32[]{:S(2)}, u32[]{:S(2)}) collective-permute-start(bf16[64,3072]{1,0:T(8,128)(2,1)S(1)} %get-tuple-element.23), channel_id=1, source_target_pairs={{0,1},{1,0},{2,3},{3,2},{4,5},{5,4},{6,7},{7,6},{8,9},{9,8},{10,11... | collective-permute-start | bytes 1179656 | tf_op jit(solution)/shard_map/ppermute | solution.py:387
  30.5 1.5 %collective-permute-start.3 = (bf16[64,1024]{1,0:T(8,128)(2,1)S(1)}, bf16[64,1024]{1,0:T(8,128)(2,1)S(1)}, u32[]{:S(2)}, u32[]{:S(2)}) collective-permute-start(bf16[64,1024]{1,0:T(8,128)(2,1)S(1)} %get-tuple-element.21), channel_id=1, source_target_pairs={{0,1},{1,0},{2,3},{3,2},{4,5},{5,4},{6,7},{7,6},{8,9},{9,8},{10,11... | collective-permute-start | bytes 393224 | tf_op jit(solution)/shard_map/ppermute | solution.py:388
  32.8 25.7 %all-to-all-start.1 = ((bf16[8,8,4096]{2,1,0:T(8,128)(2,1)}), bf16[8,8,4096]{2,1,0:T(8,128)(2,1)S(1)}, u32[]{:S(2)}, u32[]{:S(2)}) async-start(bf16[8,8,4096]{2,1,0:T(8,128)(2,1)} %bitcast.2), calls=%async_computation.1 | async-start | bytes 1048576 | tf_op jit(solution)/shard_map/all_to_all | solution.py:392
  38.8 1.9 %collective-permute-start.2 = (bf16[64,4096]{1,0:T(8,128)(2,1)S(1)}, bf16[64,4096]{1,0:T(8,128)(2,1)S(1)}, u32[]{:S(2)}, u32[]{:S(2)}) collective-permute-start(bf16[64,4096]{1,0:T(8,128)(2,1)S(1)} %bitcast.3), channel_id=1, source_target_pairs={{0,1},{1,0},{2,3},{3,2},{4,5},{5,4},{6,7},{7,6},{8,9},{9,8},{10,11... | collective-permute-start | bytes 1572872 | tf_op jit(solution)/shard_map/ppermute | solution.py:379
